TPU v7x, 32 devices: a whole 2x2x4 slice. The times are simulated.
32 devices in a mesh: replica: 4 (over y, x), fsdp: 8 (over z, core).
Axes of the slice: x: 2, y: 2, z: 4, core: 2. Of those that a mesh axis runs over, the one named last changes fastest.
Arguments:
- latents: bfloat16 [32, 256, 1152], P(('replica', 'fsdp')), may hold values from -6 to 6
- condition: bfloat16 [32, 1152], P(('replica', 'fsdp')), may hold values from -6 to 6
- bucket: int32 [32], P(('replica', 'fsdp')), may hold values from 0 to 2, as said below
- keep_slots: int32 [32, 128], P(('replica', 'fsdp')), may hold values from 0 to 255, as said below
- modulation_weight: bfloat16 [1152, 6912], P('fsdp'), may hold values from -0.1875 to 0.1875
- modulation_bias: bfloat16 [6912], P('fsdp'), may hold values from -1.5 to 1.5
- projection_weight: bfloat16 [1152, 3456], P('fsdp'), may hold values from -0.1875 to 0.1875
- query_value_bias: bfloat16 [2304], P('fsdp'), may hold values from -1.5 to 1.5
- output_weight: bfloat16 [1152, 1152], P('fsdp'), may hold values from -0.75 to 0.75
- output_bias: bfloat16 [1152], P('fsdp'), may hold values from -1.5 to 1.5
- expand_weight: bfloat16 [1152, 4608], P('fsdp'), may hold values from -0.1875 to 0.1875
- expand_bias: bfloat16 [4608], P('fsdp'), may hold values from -2.5 to 2.5
- reduce_weight: bfloat16 [4608, 1152], P('fsdp'), may hold values from -0.125 to 0.125
- reduce_bias: bfloat16 [1152], P('fsdp'), may hold values from -1.5 to 1.5
- cotangent: bfloat16 [32, 256, 1152], P(('replica', 'fsdp')), may hold values from -6 to 6
Outputs:
- block_out: bfloat16 [32, 256, 1152], P(('replica', 'fsdp'))
- grad_latents: bfloat16 [32, 256, 1152], P(('replica', 'fsdp'))
- grad_condition: float32 [32, 1152], P(('replica', 'fsdp'))
- grad_modulation_weight: float32 [1152, 6912], P('fsdp')
- grad_modulation_bias: float32 [6912], P('fsdp')
- grad_projection_weight: float32 [1152, 3456], P('fsdp')
- grad_query_value_bias: float32 [2304], P('fsdp')
- grad_output_weight: float32 [1152, 1152], P('fsdp')
- grad_output_bias: float32 [1152], P('fsdp')
- grad_expand_weight: float32 [1152, 4608], P('fsdp')
- grad_expand_bias: float32 [4608], P('fsdp')
- grad_reduce_weight: float32 [4608, 1152], P('fsdp')
- grad_reduce_bias: float32 [1152], P('fsdp')
Inputs may be any that keep to these rules, and one draw needn't show every extreme that they name: `bucket`: 0 marks a 16 x 16 grid of tokens, 1 and 2 grids of (12) x (20) and (20) x (12); an image's real tokens fill its first slots, the rest are padding. `keep_slots`: each row holds distinct slots of that image's real tokens in random order; the first live_count entries are the kept tokens, the others of the image are routed past the block.
All inputs are finite; a program needn't handle non-finite values.
Results may differ from a plain program's by a relative error of at most 0.02.
Values may be sent and summed in bfloat16 or wider, within the bound.
A program may use at most 256 MiB of HBM per device.

v0:
```python
import jax
import jax.numpy as jnp
from jax import lax
from jax.sharding import PartitionSpec as P

HEADS = 16
HEAD_DIM = 72


def layer_norm(rows_in):
    row_mean = jnp.mean(rows_in, axis=-1, keepdims=True)
    centred = rows_in - row_mean
    row_var = jnp.mean(centred * centred, axis=-1, keepdims=True)
    return centred * lax.rsqrt(row_var + 1e-06)


def modulate(rows_in, shift_part, scale_part):
    return layer_norm(rows_in) * (1.0 + scale_part) + shift_part


def gelu_tanh(values_in):
    return jax.nn.gelu(values_in, approximate=True)


def place_rows(target_rows, target_index, new_rows):
    return target_rows.at[target_index].set(new_rows, mode="drop")


def column_sums(rows_in):
    return jnp.sum(rows_in.astype(jnp.float32), axis=0)


def local(
    latents,
    condition,
    bucket,
    keep_slots,
    modulation_weight,
    modulation_bias,
    projection_weight,
    query_value_bias,
    output_weight,
    output_bias,
    expand_weight,
    expand_bias,
    reduce_weight,
    reduce_bias,
    cotangent,
):
    f32 = jnp.float32
    bf16 = jnp.bfloat16
    images, slot_count, model_width = latents.shape
    kept_rows = keep_slots.shape[1]
    row_count = images * kept_rows
    score_scale = HEAD_DIM ** (-0.5)
    shape_heads = (images, kept_rows, HEADS, HEAD_DIM)
    (
        full_mod_w,
        full_mod_b,
        full_proj_w,
        full_qv_b,
        full_out_w,
        full_out_b,
        full_exp_w,
        full_exp_b,
        full_red_w,
        full_red_b,
    ) = (
        lax.all_gather(modulation_weight, "fsdp", axis=0, tiled=True),
        lax.all_gather(modulation_bias, "fsdp", axis=0, tiled=True),
        lax.all_gather(projection_weight, "fsdp", axis=0, tiled=True),
        lax.all_gather(query_value_bias, "fsdp", axis=0, tiled=True),
        lax.all_gather(output_weight, "fsdp", axis=0, tiled=True),
        lax.all_gather(output_bias, "fsdp", axis=0, tiled=True),
        lax.all_gather(expand_weight, "fsdp", axis=0, tiled=True),
        lax.all_gather(expand_bias, "fsdp", axis=0, tiled=True),
        lax.all_gather(reduce_weight, "fsdp", axis=0, tiled=True),
        lax.all_gather(reduce_bias, "fsdp", axis=0, tiled=True),
    )
    live_count = jnp.where(bucket == 0, slot_count, slot_count - 16) // 2
    live_rows = jnp.arange(kept_rows, dtype=jnp.int32)[None, :] < live_count[:, None]
    live_float = live_rows.astype(f32)[:, :, None]
    gather_index = keep_slots[:, :, None]
    kept = jnp.take_along_axis(latents, gather_index, axis=1).astype(f32)
    cond_float = condition.astype(f32)
    cond_act = jax.nn.silu(cond_float).astype(bf16)
    modulation = jnp.dot(cond_act, full_mod_w, preferred_element_type=f32) + full_mod_b.astype(f32)
    pieces = [modulation[:, None, i * model_width : (i + 1) * model_width] for i in range(6)]
    shift_attn, scale_attn, gate_attn, shift_mlp, scale_mlp, gate_mlp = pieces
    normed_one = modulate(kept, shift_attn, scale_attn).astype(bf16).reshape(row_count, model_width)
    projected = jnp.dot(normed_one, full_proj_w, preferred_element_type=f32)
    bias_qv = full_qv_b.astype(f32)
    query_rows = (
        (projected[:, :model_width] + bias_qv[:model_width]).astype(bf16).reshape(shape_heads)
    )
    key_rows = projected[:, model_width : 2 * model_width].astype(bf16).reshape(shape_heads)
    value_rows = (
        (projected[:, 2 * model_width :] + bias_qv[model_width:]).astype(bf16).reshape(shape_heads)
    )

    def masked_scores(queries, keys_in):
        raw = (
            jnp.einsum("bqhd,bkhd->bhqk", queries, keys_in, preferred_element_type=f32)
            * score_scale
        )
        return jnp.where(live_rows[:, None, None, :], raw, -1e30)

    scores = masked_scores(query_rows, key_rows)
    row_max = jnp.max(scores, axis=-1, keepdims=True)
    row_total = jnp.sum(jnp.exp(scores - row_max), axis=-1, keepdims=True)
    log_total = row_max + jnp.log(row_total)
    probs = jnp.exp(scores - log_total)
    attended = (
        jnp.einsum("bhqk,bkhd->bqhd", probs.astype(bf16), value_rows, preferred_element_type=f32)
        .astype(bf16)
        .reshape(row_count, model_width)
    )
    branch_attn = (
        jnp.dot(attended, full_out_w, preferred_element_type=f32) + full_out_b.astype(f32)
    ).reshape(images, kept_rows, model_width)
    mixed = kept + gate_attn * branch_attn
    normed_two = modulate(mixed, shift_mlp, scale_mlp).astype(bf16).reshape(row_count, model_width)
    hidden = jnp.dot(normed_two, full_exp_w, preferred_element_type=f32) + full_exp_b.astype(f32)
    activation = gelu_tanh(hidden).astype(bf16)
    branch_mlp = (
        jnp.dot(activation, full_red_w, preferred_element_type=f32) + full_red_b.astype(f32)
    ).reshape(images, kept_rows, model_width)
    result = mixed + gate_mlp * branch_mlp
    target = jnp.where(live_rows, keep_slots, slot_count)
    block_out = jax.vmap(place_rows)(latents, target, result.astype(bf16))
    back_mod_w, back_proj_w, back_out_w, back_exp_w, back_red_w = (
        lax.all_gather(modulation_weight, "fsdp", axis=0, tiled=True),
        lax.all_gather(projection_weight, "fsdp", axis=0, tiled=True),
        lax.all_gather(output_weight, "fsdp", axis=0, tiled=True),
        lax.all_gather(expand_weight, "fsdp", axis=0, tiled=True),
        lax.all_gather(reduce_weight, "fsdp", axis=0, tiled=True),
    )
    grad_rows = jnp.take_along_axis(cotangent, gather_index, axis=1).astype(f32) * live_float
    grad_gate_mlp = jnp.sum(grad_rows * branch_mlp, axis=1)
    grad_mlp = (gate_mlp * grad_rows).astype(bf16).reshape(row_count, model_width)
    local_red_w = jnp.einsum("rm,rd->md", activation, grad_mlp, preferred_element_type=f32)
    local_red_b = column_sums(grad_mlp)
    grad_act = jnp.einsum("rd,md->rm", grad_mlp, back_red_w, preferred_element_type=f32)
    gelu_pull = jax.vjp(gelu_tanh, hidden)[1]
    grad_hidden = gelu_pull(grad_act)[0].astype(bf16)
    local_exp_w = jnp.einsum("rd,rm->dm", normed_two, grad_hidden, preferred_element_type=f32)
    local_exp_b = column_sums(grad_hidden)
    mlp_red_w, mlp_red_b, mlp_exp_w, mlp_exp_b = (
        lax.psum_scatter(
            local_red_w.astype(jnp.bfloat16), "fsdp", scatter_dimension=0, tiled=True
        ).astype(jnp.float32),
        lax.psum_scatter(
            local_red_b.astype(jnp.bfloat16), "fsdp", scatter_dimension=0, tiled=True
        ).astype(jnp.float32),
        lax.psum_scatter(
            local_exp_w.astype(jnp.bfloat16), "fsdp", scatter_dimension=0, tiled=True
        ).astype(jnp.float32),
        lax.psum_scatter(
            local_exp_b.astype(jnp.bfloat16), "fsdp", scatter_dimension=0, tiled=True
        ).astype(jnp.float32),
    )
    grad_normed_two = jnp.einsum(
        "rm,dm->rd", grad_hidden, back_exp_w, preferred_element_type=f32
    ).reshape(images, kept_rows, model_width)
    pull_two = jax.vjp(modulate, mixed, shift_mlp, scale_mlp)[1]
    grad_mixed_ln, grad_shift_mlp, grad_scale_mlp = pull_two(grad_normed_two)
    grad_mixed = grad_rows + grad_mixed_ln
    grad_gate_attn = jnp.sum(grad_mixed * branch_attn, axis=1)
    grad_attn = (gate_attn * grad_mixed).astype(bf16).reshape(row_count, model_width)
    local_out_w = jnp.einsum("rd,re->de", attended, grad_attn, preferred_element_type=f32)
    local_out_b = column_sums(grad_attn)
    grad_attended = (
        jnp.einsum("re,de->rd", grad_attn, back_out_w, preferred_element_type=f32)
        .astype(bf16)
        .reshape(shape_heads)
    )
    scores_again = masked_scores(query_rows, key_rows)
    probs_again = jnp.exp(scores_again - log_total)
    grad_values = jnp.einsum(
        "bhqk,bqhd->bkhd", probs_again.astype(bf16), grad_attended, preferred_element_type=f32
    ).astype(bf16)
    grad_probs = jnp.einsum(
        "bqhd,bkhd->bhqk", grad_attended, value_rows, preferred_element_type=f32
    )
    row_inner = jnp.sum(grad_probs * probs_again, axis=-1, keepdims=True)
    grad_scores = (probs_again * (grad_probs - row_inner)).astype(bf16)
    grad_query = (
        jnp.einsum("bhqk,bkhd->bqhd", grad_scores, key_rows, preferred_element_type=f32)
        * score_scale
    ).astype(bf16)
    grad_keys = (
        jnp.einsum("bhqk,bqhd->bkhd", grad_scores, query_rows, preferred_element_type=f32)
        * score_scale
    ).astype(bf16)
    grad_projected = jnp.concatenate(
        [
            grad_query.reshape(row_count, model_width),
            grad_keys.reshape(row_count, model_width),
            grad_values.reshape(row_count, model_width),
        ],
        axis=1,
    )
    local_proj_w = jnp.einsum("rd,re->de", normed_one, grad_projected, preferred_element_type=f32)
    local_qv_b = jnp.concatenate(
        [
            column_sums(grad_projected[:, :model_width]),
            column_sums(grad_projected[:, 2 * model_width :]),
        ]
    )
    grad_normed_one = jnp.einsum(
        "re,de->rd", grad_projected, back_proj_w, preferred_element_type=f32
    ).reshape(images, kept_rows, model_width)
    pull_one = jax.vjp(modulate, kept, shift_attn, scale_attn)[1]
    grad_kept_ln, grad_shift_attn, grad_scale_attn = pull_one(grad_normed_one)
    grad_kept = grad_mixed + grad_kept_ln
    grad_latents = jax.vmap(place_rows)(cotangent, target, grad_kept.astype(bf16))
    grad_modulation = jnp.concatenate(
        [
            grad_shift_attn[:, 0],
            grad_scale_attn[:, 0],
            grad_gate_attn,
            grad_shift_mlp[:, 0],
            grad_scale_mlp[:, 0],
            grad_gate_mlp,
        ],
        axis=1,
    ).astype(bf16)
    grad_cond_act = jnp.einsum("be,de->bd", grad_modulation, back_mod_w, preferred_element_type=f32)
    silu_pull = jax.vjp(jax.nn.silu, cond_float)[1]
    grad_condition = silu_pull(grad_cond_act)[0]
    local_mod_w = jnp.einsum("bd,be->de", cond_act, grad_modulation, preferred_element_type=f32)
    local_mod_b = column_sums(grad_modulation)
    rest_mod_w, rest_mod_b, rest_proj_w, rest_qv_b, rest_out_w, rest_out_b = (
        lax.psum_scatter(
            local_mod_w.astype(jnp.bfloat16), "fsdp", scatter_dimension=0, tiled=True
        ).astype(jnp.float32),
        lax.psum_scatter(
            local_mod_b.astype(jnp.bfloat16), "fsdp", scatter_dimension=0, tiled=True
        ).astype(jnp.float32),
        lax.psum_scatter(
            local_proj_w.astype(jnp.bfloat16), "fsdp", scatter_dimension=0, tiled=True
        ).astype(jnp.float32),
        lax.psum_scatter(
            local_qv_b.astype(jnp.bfloat16), "fsdp", scatter_dimension=0, tiled=True
        ).astype(jnp.float32),
        lax.psum_scatter(
            local_out_w.astype(jnp.bfloat16), "fsdp", scatter_dimension=0, tiled=True
        ).astype(jnp.float32),
        lax.psum_scatter(
            local_out_b.astype(jnp.bfloat16), "fsdp", scatter_dimension=0, tiled=True
        ).astype(jnp.float32),
    )
    shares = (
        lax.psum_scatter(
            rest_mod_w.astype(jnp.bfloat16), "replica", scatter_dimension=1, tiled=True
        ).astype(jnp.float32),
        lax.psum_scatter(
            rest_proj_w.astype(jnp.bfloat16), "replica", scatter_dimension=1, tiled=True
        ).astype(jnp.float32),
        lax.psum_scatter(
            rest_out_w.astype(jnp.bfloat16), "replica", scatter_dimension=1, tiled=True
        ).astype(jnp.float32),
        lax.psum_scatter(
            mlp_exp_w.astype(jnp.bfloat16), "replica", scatter_dimension=1, tiled=True
        ).astype(jnp.float32),
        lax.psum_scatter(
            mlp_red_w.astype(jnp.bfloat16), "replica", scatter_dimension=1, tiled=True
        ).astype(jnp.float32),
    )
    sum_mod_w, sum_proj_w, sum_out_w, sum_exp_w, sum_red_w = (
        lax.all_gather(shares[0].astype(jnp.bfloat16), "replica", axis=1, tiled=True).astype(
            jnp.float32
        ),
        lax.all_gather(shares[1].astype(jnp.bfloat16), "replica", axis=1, tiled=True).astype(
            jnp.float32
        ),
        lax.all_gather(shares[2].astype(jnp.bfloat16), "replica", axis=1, tiled=True).astype(
            jnp.float32
        ),
        lax.all_gather(shares[3].astype(jnp.bfloat16), "replica", axis=1, tiled=True).astype(
            jnp.float32
        ),
        lax.all_gather(shares[4].astype(jnp.bfloat16), "replica", axis=1, tiled=True).astype(
            jnp.float32
        ),
    )
    sum_mod_b, sum_qv_b, sum_out_b, sum_exp_b, sum_red_b = lax.psum(
        (rest_mod_b, rest_qv_b, rest_out_b, mlp_exp_b, mlp_red_b), "replica"
    )
    return (
        block_out,
        grad_latents,
        grad_condition,
        sum_mod_w,
        sum_mod_b,
        sum_proj_w,
        sum_qv_b,
        sum_out_w,
        sum_out_b,
        sum_exp_w,
        sum_exp_b,
        sum_red_w,
        sum_red_b,
    )


def solution(mesh):
    placed = (
        P(("replica", "fsdp"), None, None),
        P(("replica", "fsdp"), None),
        P(("replica", "fsdp")),
        P(("replica", "fsdp"), None),
        P("fsdp", None),
        P("fsdp"),
        P("fsdp", None),
        P("fsdp"),
        P("fsdp", None),
        P("fsdp"),
        P("fsdp", None),
        P("fsdp"),
        P("fsdp", None),
        P("fsdp"),
        P(("replica", "fsdp"), None, None),
    )
    return jax.shard_map(
        local,
        mesh=mesh,
        in_specs=placed,
        out_specs=(
            P(("replica", "fsdp"), None, None),
            P(("replica", "fsdp"), None, None),
            P(("replica", "fsdp"), None),
            P("fsdp", None),
            P("fsdp"),
            P("fsdp", None),
            P("fsdp"),
            P("fsdp", None),
            P("fsdp"),
            P("fsdp", None),
            P("fsdp"),
            P("fsdp", None),
            P("fsdp"),
        ),
        check_vma=False,
    )
```

profile of v0, /device:TPU:0, one launch (start us, length us, event | category | flops | bytes accessed | tf_op | source)
XLA Modules:
  0.0 1305.8 jit_solution(7844802750100305167)
XLA Ops:
  17.3 32.9 %all-reduce.12 = (bf16[2304]{0:T(1024)(128)(2,1)S(1)}, bf16[6912]{0:T(1024)(128)(2,1)S(1)}, bf16[4608]{0:T(1024)(128)(2,1)S(1)}, bf16[1152]{0:T(1024)(128)(2,1)S(1)}, bf16[1152]{0:T(1024)(128)(2,1)S(1)}) all-reduce(bf16[2304]{0:T(1024)(128)(2,1)S(1)} %dynamic-update-slice.1, ...), channel_id=1, replica_groups=mesh['replica'=4,'fsdp'=8] {'fsdp'}, use_global_device_ids=true, to_apply=%add.1 | all-reduce | flops 16128 | bytes 64512
  53.1 104.4 %all-gather.12.cloned.1.call-done = bf16[1152,6912]{1,0:T(8,128)(2,1)} async-done(((bf16[144,6912]{1,0:T(8,128)(2,1)}), bf16[1152,6912]{1,0:T(8,128)(2,1)}) %all-gather.12.cloned.1.call-update) | async-done | bytes 15925264 | tf_op jit(solution)/shard_map/all_gather | solution.py:69
  165.4 70.6 %all-gather.14.cloned.1.call-done = bf16[1152,3456]{1,0:T(8,128)(2,1)} async-done(((bf16[144,3456]{1,0:T(8,128)(2,1)}), bf16[1152,3456]{1,0:T(8,128)(2,1)}) %all-gather.14.cloned.1.call-update) | async-done | bytes 7962640 | tf_op jit(solution)/shard_map/all_gather | solution.py:71
  244.9 25.5 %all-gather.16.cloned.1.call-done = bf16[1152,1152]{1,0:T(8,128)(2,1)} async-done(((bf16[144,1152]{1,0:T(8,128)(2,1)}), bf16[1152,1152]{1,0:T(8,128)(2,1)}) %all-gather.16.cloned.1.call-update) | async-done | bytes 2654224 | tf_op jit(solution)/shard_map/all_gather | solution.py:73
  273.9 97.4 %all-gather.18.cloned.1.call-done = bf16[1152,4608]{1,0:T(8,128)(2,1)} async-done(((bf16[144,4608]{1,0:T(8,128)(2,1)}), bf16[1152,4608]{1,0:T(8,128)(2,1)}) %all-gather.18.cloned.1.call-update) | async-done | bytes 10616848 | tf_op jit(solution)/shard_map/all_gather | solution.py:75
  378.6 93.2 %all-gather.20.cloned.1.call-done = bf16[4608,1152]{1,0:T(8,128)(2,1)} async-done(((bf16[576,1152]{1,0:T(8,128)(2,1)}), bf16[4608,1152]{1,0:T(8,128)(2,1)}) %all-gather.20.cloned.1.call-update) | async-done | bytes 10616848 | tf_op jit(solution)/shard_map/all_gather | solution.py:77
  471.8 8.6 fusion.77
  487.4 8.9 convolution_convert_fusion
  523.0 8.0 fusion.24
  549.8 46.8 %reduce-scatter.27.cloned.1.call-done = bf16[144,4608]{1,0:T(8,128)(2,1)} async-done(((bf16[1152,4608]{1,0:T(8,128)(2,1)}), bf16[144,4608]{1,0:T(8,128)(2,1)}) %reduce-scatter.27.cloned.1.call-update) | async-done | bytes 1327120 | tf_op jit(solution)/shard_map/reduce_scatter | solution.py:155
  600.4 107.6 %reduce-scatter.29.cloned.1.call-done = bf16[576,1152]{1,0:T(8,128)(2,1)} async-done(((bf16[4608,1152]{1,0:T(8,128)(2,1)}), bf16[576,1152]{1,0:T(8,128)(2,1)}) %reduce-scatter.29.cloned.1.call-update) | async-done | bytes 1327120 | tf_op jit(solution)/shard_map/reduce_scatter | solution.py:149
  710.7 158.8 %reduce-scatter.21.cloned.1.call-done = bf16[144,6912]{1,0:T(8,128)(2,1)} async-done(((bf16[1152,6912]{1,0:T(8,128)(2,1)}), bf16[144,6912]{1,0:T(8,128)(2,1)}) %reduce-scatter.21.cloned.1.call-update) | async-done | bytes 1990672 | tf_op jit(solution)/shard_map/reduce_scatter | solution.py:234
  874.1 34.5 %reduce-scatter.25.cloned.1.call-done = bf16[144,1152]{1,0:T(8,128)(2,1)} async-done(((bf16[1152,1152]{1,0:T(8,128)(2,1)}), bf16[144,1152]{1,0:T(8,128)(2,1)}) %reduce-scatter.25.cloned.1.call-update) | async-done | bytes 331792 | tf_op jit(solution)/shard_map/reduce_scatter | solution.py:246
  910.7 85.1 %reduce-scatter.23.cloned.1.call-done = bf16[144,3456]{1,0:T(8,128)(2,1)} async-done(((bf16[1152,3456]{1,0:T(8,128)(2,1)}), bf16[144,3456]{1,0:T(8,128)(2,1)}) %reduce-scatter.23.cloned.1.call-update) | async-done | bytes 995344 | tf_op jit(solution)/shard_map/reduce_scatter | solution.py:240
  998.4 36.8 %reduce-scatter.37.cloned.1.call-done = bf16[1152,144]{1,0:T(8,128)(2,1)} async-done(((bf16[4608,144]{1,0:T(8,128)(2,1)}), bf16[1152,144]{1,0:T(8,128)(2,1)}) %reduce-scatter.37.cloned.1.call-update) | async-done | bytes 331792
  1037.3 31.1 %reduce-scatter.39.cloned.1.call-done = bf16[288,576]{1,0:T(8,128)(2,1)} async-done(((bf16[1152,576]{1,0:T(8,128)(2,1)}), bf16[288,576]{1,0:T(8,128)(2,1)}) %reduce-scatter.39.cloned.1.call-update) | async-done | bytes 331792
  1068.5 51.1 %reduce-scatter.31.cloned.1.call-done = bf16[1728,144]{1,0:T(8,128)(2,1)} async-done(((bf16[6912,144]{1,0:T(8,128)(2,1)}), bf16[1728,144]{1,0:T(8,128)(2,1)}) %reduce-scatter.31.cloned.1.call-update) | async-done | bytes 497680
  1129.4 29.0 %all-reduce.11 = (bf16[6912]{0:T(1024)(128)(2,1)S(1)}, bf16[2304]{0:T(1024)(128)(2,1)S(1)}, bf16[1152]{0:T(1024)(128)(2,1)S(1)}, bf16[4608]{0:T(1024)(128)(2,1)S(1)}, bf16[1152]{0:T(1024)(128)(2,1)S(1)}) all-reduce(bf16[6912]{0:T(1024)(128)(2,1)S(1)} %dynamic-update-slice.10, ...), channel_id=4, replica_groups=mesh['replica'=4,'fsdp'=8] {'fsdp'}, use_global_device_ids=true, to_apply=%region_21.23.clone | all-reduce | flops 16128 | bytes 64512
  1158.7 15.9 %all-reduce.10 = (f32[864]{0:T(1024)}, f32[288]{0:T(512)}, f32[144]{0:T(256)}, f32[576]{0:T(1024)}, f32[144]{0:T(256)}) all-reduce(f32[864]{0:T(1024)S(1)} %dynamic-slice_convert_fusion.1, f32[288]{0:T(512)S(1)} %dynamic-slice_convert_fusion.2, f32[144]{0:T(256)S(1)} %get-tuple-element.86, ...), channel_id=1, replica_groups=mesh['replica'=4,'fsdp'=8] {'replica'}, use_global_device_ids=true, to_apply=%region_22.24 | all-reduce | flops 2016 | bytes 16128 | tf_op jit(solution)/shard_map/psum | solution.py:287
  1174.6 10.6 fusion.50
  1186.3 10.4 all-gather.2
  1199.3 11.5 all-gather.1
  1222.1 28.8 %all-gather.24.cloned.1.call-done = bf16[576,1152]{0,1:T(8,128)(2,1)} async-done(((bf16[576,288]{0,1:T(8,128)(2,1)}), bf16[576,1152]{0,1:T(8,128)(2,1)}) %all-gather.24.cloned.1.call-update) | async-done | bytes 1327120 | tf_op jit(solution)/shard_map/all_gather | solution.py:283
  1253.8 34.4 %all-gather.26.cloned.1.call-done = bf16[4,1728,144]{1,2,0:T(8,128)(2,1)} async-done(((bf16[1,1728,144]{1,2,0:T(8,128)(2,1)}), bf16[4,1728,144]{1,2,0:T(8,128)(2,1)}) %all-gather.26.cloned.1.call-update) | async-done | bytes 1990672 | tf_op jit(solution)/shard_map/all_gather | solution.py:271
  (213 shorter events, 142.8 us)
Async XLA Ops:
  7.2 150.3 %all-gather.12.cloned.1.call-start = ((), (), s32[]{:S(2)}) async-start(), calls=%async_computation.10 | async-start | bytes 17915904 | tf_op jit(solution)/shard_map/all_gather | solution.py:69
  9.5 40.7 %copy-start.31 = (s32[1,128]{1,0:T(1,128)S(1)}, s32[1,128]{1,0:T(1,128)}, u32[]{:S(2)}) copy-start(s32[1,128]{1,0:T(1,128)} %param.20) | copy-start | bytes 1540
  9.5 226.5 %all-gather.14.cloned.1.call-start = ((), (), s32[]{:S(2)}) async-start(), calls=%async_computation.11 | async-start | bytes 8957952 | tf_op jit(solution)/shard_map/all_gather | solution.py:71
  10.2 260.2 %all-gather.16.cloned.1.call-start = ((), (), s32[]{:S(2)}) async-start(), calls=%async_computation.12 | async-start | bytes 2985984 | tf_op jit(solution)/shard_map/all_gather | solution.py:73
  11.0 360.4 %all-gather.18.cloned.1.call-start = ((), (), s32[]{:S(2)}) async-start(), calls=%async_computation.13 | async-start | bytes 11943936 | tf_op jit(solution)/shard_map/all_gather | solution.py:75
  11.5 460.2 %all-gather.20.cloned.1.call-start = ((), (), s32[]{:S(2)}) async-start(), calls=%async_computation.14 | async-start | bytes 11943936 | tf_op jit(solution)/shard_map/all_gather | solution.py:77
  12.1 584.4 %reduce-scatter.27.cloned.1.call-start = ((), (), s32[]{:S(2)}) async-start(), calls=%async_computation.18 | async-start | bytes 11943936 | tf_op jit(solution)/shard_map/reduce_scatter | solution.py:155
  242.2 28.2 %copy-start.11 = (bf16[128,1152]{0,1:T(8,128)(2,1)}, bf16[128,1152]{0,1:T(8,128)(2,1)S(1)}, u32[]{:S(2)}) copy-start(bf16[128,1152]{0,1:T(8,128)(2,1)S(1)} %copy.63) | copy-start | bytes 884740
  273.9 104.7 %copy-start.27 = (f32[128]{0:T(128)}, f32[128]{0:T(128)S(1)}, u32[]{:S(2)}) copy-start(f32[128]{0:T(128)S(1)} %multiply_reduce_fusion.1) | copy-start | bytes 1540
  487.4 220.6 %reduce-scatter.29.cloned.1.call-start = ((), (), s32[]{:S(2)}) async-start(), calls=%async_computation.20 | async-start | bytes 11943936 | tf_op jit(solution)/shard_map/reduce_scatter | solution.py:149
  496.4 373.1 %reduce-scatter.21.cloned.1.call-start = ((), (), s32[]{:S(2)}) async-start(), calls=%async_computation.15 | async-start | bytes 17915904 | tf_op jit(solution)/shard_map/reduce_scatter | solution.py:234
  538.6 370.0 %reduce-scatter.25.cloned.1.call-start = ((), (), s32[]{:S(2)}) async-start(), calls=%async_computation.17 | async-start | bytes 2985984 | tf_op jit(solution)/shard_map/reduce_scatter | solution.py:246
  542.8 452.9 %reduce-scatter.23.cloned.1.call-start = ((), (), s32[]{:S(2)}) async-start(), calls=%async_computation.16 | async-start | bytes 8957952 | tf_op jit(solution)/shard_map/reduce_scatter | solution.py:240
  549.7 485.4 %reduce-scatter.37.cloned.1.call-start = ((), (), s32[]{:S(2)}) async-start(), calls=%async_computation.26 | async-start | bytes 2949120
  600.3 468.0 %reduce-scatter.39.cloned.1.call-start = ((), (), s32[]{:S(2)}) async-start(), calls=%async_computation.27 | async-start | bytes 1843200
  710.6 409.0 %reduce-scatter.31.cloned.1.call-start = ((), (), s32[]{:S(2)}) async-start(), calls=%async_computation.23 | async-start | bytes 4423680
  874.0 311.2 %reduce-scatter.35.cloned.1.call-start = ((), (), s32[]{:S(2)}) async-start(), calls=%async_computation.25 | async-start | bytes 737280
  910.7 287.4 %reduce-scatter.33.cloned.1.call-start = ((), (), s32[]{:S(2)}) async-start(), calls=%async_computation.24 | async-start | bytes 2211840
  998.3 126.1 %copy-start.32 = (s32[1,128]{1,0:T(1,128)S(1)}, s32[1,128]{1,0:T(1,128)}, u32[]{:S(2)}) copy-start(s32[1,128]{1,0:T(1,128)} %param.20) | copy-start | bytes 1540
  998.4 220.6 %all-gather.22.cloned.1.call-start = ((), (), s32[]{:S(2)}) async-start(), calls=%async_computation.19 | async-start | bytes 1658880 | tf_op jit(solution)/shard_map/all_gather | solution.py:280
  1037.2 213.7 %all-gather.24.cloned.1.call-start = ((), (), s32[]{:S(2)}) async-start(), calls=%async_computation.21 | async-start | bytes 1843200 | tf_op jit(solution)/shard_map/all_gather | solution.py:283
  1068.4 219.8 %all-gather.26.cloned.1.call-start = ((), (), s32[]{:S(2)}) async-start(), calls=%async_computation.22 | async-start | bytes 2580480 | tf_op jit(solution)/shard_map/all_gather | solution.py:271
  1126.5 58.7 %copy-start.1 = (bf16[256,1152]{1,0:T(8,128)(2,1)}, bf16[256,1152]{1,0:T(8,128)(2,1)S(1)}, u32[]{:S(2)}) copy-start(bf16[256,1152]{1,0:T(8,128)(2,1)S(1)} %scatter_custom_fusion) | copy-start | bytes 1769476
  1129.1 56.1 %copy-start = (bf16[256,1152]{1,0:T(8,128)(2,1)}, bf16[256,1152]{1,0:T(8,128)(2,1)S(1)}, u32[]{:S(2)}) copy-start(bf16[256,1152]{1,0:T(8,128)(2,1)S(1)} %scatter_custom_fusion.1) | copy-start | bytes 1769476
  (27 other events, 122.3 us)
Sparse Core Ops, SparseCore 0:
  9.7 147.8 all-gather.11
  159.2 76.7 all-gather.13
  237.6 32.7 all-gather.15
  271.9 99.4 all-gather.17
  372.9 98.8 all-gather.19
  487.5 108.9 reduce-scatter.26
  599.0 108.9 reduce-scatter.28
  710.4 159.0 reduce-scatter.20
  872.5 36.0 reduce-scatter.24
  910.9 84.8 reduce-scatter.22
  999.4 35.7 reduce-scatter.36
  1038.0 30.3 reduce-scatter.38
  1072.3 47.2 reduce-scatter.30
  1123.1 25.0 reduce-scatter.34
  1151.7 33.2 reduce-scatter.32
  1187.3 31.6 all-gather.21
  1220.7 30.1 all-gather.23
  1253.2 35.0 all-gather.25
where the time goes:
time: 1310 us
  waiting for transfers between devices  1010 us (77%)
  blocking collectives  99.6 us (8%)
  matrix products  97.2 us (7%)
  local copies, waits for them, and re-layouts  55.6 us (4%)
  between operations  21 us (2%)
  other arithmetic  17.3 us (1%)
    reduce_scatter x1, waiting for transfers between devices, local(): lax.psum_scatter(local_mod_w.astype(jnp.bfloat16), 'fsdp', scatter_dimens...  159 us
    unnamed x23, waiting for transfers between devices  122 us
    reduce_scatter x1, waiting for transfers between devices, local(): lax.psum_scatter(local_red_w.astype(jnp.bfloat16), 'fsdp', scatter_dimens...  108 us
    all_gather x1, waiting for transfers between devices, local(): lax.all_gather(modulation_weight, 'fsdp', axis=0, tiled=True)  104 us
    all_gather x1, waiting for transfers between devices, local(): lax.all_gather(expand_weight, 'fsdp', axis=0, tiled=True)  97.4 us
    all_gather x1, waiting for transfers between devices, local(): lax.all_gather(reduce_weight, 'fsdp', axis=0, tiled=True)  93.2 us
    reduce_scatter x1, waiting for transfers between devices, local(): lax.psum_scatter(local_proj_w.astype(jnp.bfloat16), 'fsdp', scatter_dimen...  85.1 us
    all_gather x1, waiting for transfers between devices, local(): lax.all_gather(projection_weight, 'fsdp', axis=0, tiled=True)  70.6 us
  transfers between devices with their start and end apart: 18, of which 16 were waited for; matrix products, arithmetic and copies ran while one was open for 11% of the time, Pallas kernels for 0%

commit v1 on v0

--- a/solution.py
+++ b/solution.py
@@ -5,6 +5,18 @@
 
 HEADS = 16
 HEAD_DIM = 72
+
+
+def collect(value, axis, dim):
+    ways, here, step = (lax.axis_size(axis), lax.axis_index(axis), value.shape[dim])
+    line, have = (value, 1)
+    while have < ways:
+        line = jnp.concatenate(
+            [line, lax.ppermute(line, axis, [(d, (d - have) % ways) for d in range(ways)])],
+            axis=dim,
+        )
+        have = 2 * have
+    return jnp.roll(line, here * step, axis=dim)
 
 
 def layer_norm(rows_in):
@@ -66,7 +78,7 @@
         full_red_w,
         full_red_b,
     ) = (
-        lax.all_gather(modulation_weight, "fsdp", axis=0, tiled=True),
+        collect(modulation_weight, "fsdp", 0),
         lax.all_gather(modulation_bias, "fsdp", axis=0, tiled=True),
         lax.all_gather(projection_weight, "fsdp", axis=0, tiled=True),
         lax.all_gather(query_value_bias, "fsdp", axis=0, tiled=True),

time: 1310 us -> 1780 us (1.36)
  blocking collectives: 99.6 us -> 596 us
  waiting for transfers between devices: 1010 us -> 948 us
  local copies, waits for them, and re-layouts: 55.6 us -> 85 us
    unnamed x2, blocking collectives: 61.9 us -> 553 us
    ppermute x0 -> x3, waiting for transfers between devices: none -> 189 us  [collect(): lax.ppermute(line, axis, [(d, (d - have) % ways) for d in range(ways)])]
    all_gather x1, waiting for transfers between devices: 97.4 us -> 0.02 us  [local(): lax.all_gather(expand_weight, 'fsdp', axis=0, tiled=True)]
    all_gather x1, waiting for transfers between devices: 93.2 us -> 0.02 us  [local(): lax.all_gather(reduce_weight, 'fsdp', axis=0, tiled=True)]
    all_gather x1, waiting for transfers between devices: 70.6 us -> 0.02 us  [local(): lax.all_gather(projection_weight, 'fsdp', axis=0, tiled=True)]
    reduce_scatter x1, waiting for transfers between devices: 46.8 us -> 109 us  [local(): lax.psum_scatter(local_exp_w.astype(jnp.bfloat16), 'fsdp', scatter_dimens...]
    reduce_scatter x1, waiting for transfers between devices: 108 us -> 45.9 us  [local(): lax.psum_scatter(local_red_w.astype(jnp.bfloat16), 'fsdp', scatter_dimens...]
    all_gather x1, waiting for transfers between devices: 25.5 us -> 0.02 us  [local(): lax.all_gather(output_weight, 'fsdp', axis=0, tiled=True)]
  transfers between devices with their start and end apart: 18 -> 21, of which waited for: 16 -> 15; matrix products, arithmetic and copies ran while one was open for 11% -> 10% of each run, Pallas kernels for 0% -> 0%
where the time goes in v1:
time: 1780 us
  waiting for transfers between devices  948 us (53%)
  blocking collectives  596 us (33%)
  matrix products  89.9 us (5%)
  local copies, waits for them, and re-layouts  85 us (5%)
  other arithmetic  25.4 us (1%)
  between operations  21.4 us (1%)
    unnamed x2, blocking collectives  553 us
    ppermute x3, waiting for transfers between devices, collect(): lax.ppermute(line, axis, [(d, (d - have) % ways) for d in range(ways)])  189 us
    reduce_scatter x1, waiting for transfers between devices, local(): lax.psum_scatter(local_mod_w.astype(jnp.bfloat16), 'fsdp', scatter_dimens...  158 us
    unnamed x23, waiting for transfers between devices  145 us
    reduce_scatter x1, waiting for transfers between devices, local(): lax.psum_scatter(local_exp_w.astype(jnp.bfloat16), 'fsdp', scatter_dimens...  109 us
    all_gather x1, waiting for transfers between devices, local(): lax.all_gather(modulation_weight, 'fsdp', axis=0, tiled=True)  108 us
    reduce_scatter x1, waiting for transfers between devices, local(): lax.psum_scatter(local_proj_w.astype(jnp.bfloat16), 'fsdp', scatter_dimen...  84.7 us
    unnamed x125, local copies, waits for them, and re-layouts  57.9 us
  transfers between devices with their start and end apart: 21, of which 15 were waited for; matrix products, arithmetic and copies ran while one was open for 10% of the time, Pallas kernels for 0%

profile of v1, /device:TPU:0, one launch (start us, length us, event | category | flops | bytes accessed | tf_op | source)
XLA Modules:
  0.0 1775.8 jit_solution(13372790501989748450)
XLA Ops:
  15.6 56.1 %collective-permute-done = bf16[144,6912]{1,0:T(8,128)(2,1)S(1)} collective-permute-done((bf16[144,6912]{1,0:T(8,128)(2,1)S(1)}, bf16[144,6912]{1,0:T(8,128)(2,1)S(1)}, u32[]{:S(2)}, u32[]{:S(2)}) %collective-permute-start) | collective-permute-done | bytes 1990688 | tf_op jit(solution)/shard_map/ppermute | solution.py:15
  74.4 132.6 %collective-permute-done.1 = bf16[288,6912]{1,0:T(8,128)(2,1)} collective-permute-done((bf16[288,6912]{1,0:T(8,128)(2,1)}, bf16[288,6912]{1,0:T(8,128)(2,1)}, u32[]{:S(2)}, u32[]{:S(2)}) %collective-permute-start.1) | collective-permute-done | bytes 3981344 | tf_op jit(solution)/shard_map/ppermute | solution.py:15
  222.0 524.5 %all-reduce.12 = (bf16[2304]{0:T(1024)(128)(2,1)S(1)}, bf16[6912]{0:T(1024)(128)(2,1)S(1)}, bf16[4608]{0:T(1024)(128)(2,1)S(1)}, bf16[1152]{0:T(1024)(128)(2,1)S(1)}, bf16[1152]{0:T(1024)(128)(2,1)}) all-reduce(bf16[2304]{0:T(1024)(128)(2,1)S(1)} %dynamic-update-slice.1, ...), channel_id=1, replica_groups=mesh['replica'=4,'fsdp'=8] {'fsdp'}, use_global_device_ids=true, to_apply=%add.1 | all-reduce | flops 16128 | bytes 64512
  778.8 9.3 fusion.12
  811.7 8.6 fusion.83
  827.8 8.0 fusion.30
  877.3 45.9 %reduce-scatter.29.cloned.1.call-done = bf16[576,1152]{1,0:T(8,128)(2,1)} async-done(((bf16[4608,1152]{1,0:T(8,128)(2,1)}), bf16[576,1152]{1,0:T(8,128)(2,1)}) %reduce-scatter.29.cloned.1.call-update) | async-done | bytes 1327120 | tf_op jit(solution)/shard_map/reduce_scatter | solution.py:161
  925.9 108.7 %reduce-scatter.27.cloned.1.call-done = bf16[144,4608]{1,0:T(8,128)(2,1)} async-done(((bf16[1152,4608]{1,0:T(8,128)(2,1)}), bf16[144,4608]{1,0:T(8,128)(2,1)}) %reduce-scatter.27.cloned.1.call-update) | async-done | bytes 1327120 | tf_op jit(solution)/shard_map/reduce_scatter | solution.py:167
  1038.4 157.7 %reduce-scatter.21.cloned.1.call-done = bf16[144,6912]{1,0:T(8,128)(2,1)} async-done(((bf16[1152,6912]{1,0:T(8,128)(2,1)}), bf16[144,6912]{1,0:T(8,128)(2,1)}) %reduce-scatter.21.cloned.1.call-update) | async-done | bytes 1990672 | tf_op jit(solution)/shard_map/reduce_scatter | solution.py:246
  1200.6 34.5 %reduce-scatter.25.cloned.1.call-done = bf16[144,1152]{1,0:T(8,128)(2,1)} async-done(((bf16[1152,1152]{1,0:T(8,128)(2,1)}), bf16[144,1152]{1,0:T(8,128)(2,1)}) %reduce-scatter.25.cloned.1.call-update) | async-done | bytes 331792 | tf_op jit(solution)/shard_map/reduce_scatter | solution.py:258
  1237.8 84.7 %reduce-scatter.23.cloned.1.call-done = bf16[144,3456]{1,0:T(8,128)(2,1)} async-done(((bf16[1152,3456]{1,0:T(8,128)(2,1)}), bf16[144,3456]{1,0:T(8,128)(2,1)}) %reduce-scatter.23.cloned.1.call-update) | async-done | bytes 995344 | tf_op jit(solution)/shard_map/reduce_scatter | solution.py:252
  1325.2 28.9 %reduce-scatter.39.cloned.1.call-done = bf16[288,576]{1,0:T(8,128)(2,1)} async-done(((bf16[1152,576]{1,0:T(8,128)(2,1)}), bf16[288,576]{1,0:T(8,128)(2,1)}) %reduce-scatter.39.cloned.1.call-update) | async-done | bytes 331792
  1354.1 41.3 %reduce-scatter.37.cloned.1.call-done = bf16[1152,144]{1,0:T(8,128)(2,1)} async-done(((bf16[4608,144]{1,0:T(8,128)(2,1)}), bf16[1152,144]{1,0:T(8,128)(2,1)}) %reduce-scatter.37.cloned.1.call-update) | async-done | bytes 331792
  1397.5 49.0 %reduce-scatter.31.cloned.1.call-done = bf16[1728,144]{1,0:T(8,128)(2,1)} async-done(((bf16[6912,144]{1,0:T(8,128)(2,1)}), bf16[1728,144]{1,0:T(8,128)(2,1)}) %reduce-scatter.31.cloned.1.call-update) | async-done | bytes 497680
  1456.0 29.0 %all-reduce.11 = (bf16[6912]{0:T(1024)(128)(2,1)S(1)}, bf16[2304]{0:T(1024)(128)(2,1)S(1)}, bf16[1152]{0:T(1024)(128)(2,1)S(1)}, bf16[4608]{0:T(1024)(128)(2,1)S(1)}, bf16[1152]{0:T(1024)(128)(2,1)S(1)}) all-reduce(bf16[6912]{0:T(1024)(128)(2,1)S(1)} %dynamic-update-slice.10, ...), channel_id=4, replica_groups=mesh['replica'=4,'fsdp'=8] {'fsdp'}, use_global_device_ids=true, to_apply=%region_21.23.clone | all-reduce | flops 16128 | bytes 64512
  1485.3 15.6 all-reduce.10
  1501.9 9.7 all-gather.2
  1513.0 107.9 %all-gather.20.cloned.1.call-done = bf16[1152,6912]{1,0:T(8,128)(2,1)} async-done(((bf16[144,6912]{1,0:T(8,128)(2,1)}), bf16[1152,6912]{1,0:T(8,128)(2,1)}) %all-gather.20.cloned.1.call-update) | async-done | bytes 15925264 | tf_op jit(solution)/shard_map/all_gather | solution.py:144
  1620.9 10.3 fusion.55
  1631.2 23.8 %reduce-scatter.33.cloned.1.call-done = bf16[864,144]{1,0:T(8,128)(2,1)} async-done(((bf16[3456,144]{1,0:T(8,128)(2,1)}), bf16[864,144]{1,0:T(8,128)(2,1)}) %reduce-scatter.33.cloned.1.call-update) | async-done | bytes 248848
  1656.3 17.7 all-gather.1
  1676.7 12.7 all-gather.24.cloned.1.call-done
  1692.3 28.3 %all-gather.22.cloned.1.call-done = bf16[144,4608]{1,0:T(8,128)(2,1)} async-done(((bf16[144,1152]{1,0:T(8,128)(2,1)}), bf16[144,4608]{1,0:T(8,128)(2,1)}) %all-gather.22.cloned.1.call-update) | async-done | bytes 1327120 | tf_op jit(solution)/shard_map/all_gather | solution.py:292
  1723.7 34.3 %all-gather.26.cloned.1.call-done = bf16[4,1728,144]{1,2,0:T(8,128)(2,1)} async-done(((bf16[1,1728,144]{1,2,0:T(8,128)(2,1)}), bf16[4,1728,144]{1,2,0:T(8,128)(2,1)}) %all-gather.26.cloned.1.call-update) | async-done | bytes 1990672 | tf_op jit(solution)/shard_map/all_gather | solution.py:283
  (253 shorter events, 175.5 us)
Async XLA Ops:
  7.2 781.1 %all-gather.12.cloned.1.call-start = ((), (), s32[]{:S(2)}) async-start(), calls=%async_computation.10 | async-start | bytes 8957952 | tf_op jit(solution)/shard_map/all_gather | solution.py:83
  9.5 738.0 %copy-start.4 = (bf16[1,256,1152]{2,1,0:T(8,128)(2,1)}, bf16[1,256,1152]{2,1,0:T(8,128)(2,1)S(1)}, u32[]{:S(2)}) copy-start(bf16[1,256,1152]{2,1,0:T(8,128)(2,1)S(1)} %copy.112) | copy-start | bytes 1769476
  9.5 785.3 %all-gather.14.cloned.1.call-start = ((), (), s32[]{:S(2)}) async-start(), calls=%async_computation.11 | async-start | bytes 2985984 | tf_op jit(solution)/shard_map/all_gather | solution.py:85
  10.3 788.0 %all-gather.16.cloned.1.call-start = ((), (), s32[]{:S(2)}) async-start(), calls=%async_computation.12 | async-start | bytes 11943936 | tf_op jit(solution)/shard_map/all_gather | solution.py:87
  11.0 800.7 %all-gather.18.cloned.1.call-start = ((), (), s32[]{:S(2)}) async-start(), calls=%async_computation.13 | async-start | bytes 11943936 | tf_op jit(solution)/shard_map/all_gather | solution.py:89
  11.1 60.6 %collective-permute-start = (bf16[144,6912]{1,0:T(8,128)(2,1)S(1)}, bf16[144,6912]{1,0:T(8,128)(2,1)S(1)}, u32[]{:S(2)}, u32[]{:S(2)}) collective-permute-start(bf16[144,6912]{1,0:T(8,128)(2,1)S(1)} %copy-done), channel_id=1, source_target_pairs={{0,7},{1,0},{2,1},{3,2},{4,3},{5,4},{6,5},{7,6},{8,15},{9,8},{10,9... | collective-permute-start | bytes 5971976 | tf_op jit(solution)/shard_map/ppermute | solution.py:15
  74.3 132.8 %collective-permute-start.1 = (bf16[288,6912]{1,0:T(8,128)(2,1)}, bf16[288,6912]{1,0:T(8,128)(2,1)}, u32[]{:S(2)}, u32[]{:S(2)}) collective-permute-start(bf16[288,6912]{1,0:T(8,128)(2,1)} %pad_maximum_fusion.1), channel_id=1, source_target_pairs={{0,6},{1,7},{2,0},{3,1},{4,2},{5,3},{6,4},{7,5},{8,14},{9,15},{10,... | collective-permute-start | bytes 11943944 | tf_op jit(solution)/shard_map/ppermute | solution.py:15
  74.4 672.2 %copy-start.43 = (s32[1,128]{1,0:T(1,128)S(1)}, s32[1,128]{1,0:T(1,128)}, u32[]{:S(2)}) copy-start(s32[1,128]{1,0:T(1,128)} %param.20) | copy-start | bytes 1540
  74.4 848.8 %reduce-scatter.29.cloned.1.call-start = ((), (), s32[]{:S(2)}) async-start(), calls=%async_computation.20 | async-start | bytes 11943936 | tf_op jit(solution)/shard_map/reduce_scatter | solution.py:161
  213.5 544.3 %collective-permute-start.2 = (bf16[576,6912]{1,0:T(8,128)(2,1)}, bf16[576,6912]{1,0:T(8,128)(2,1)}, u32[]{:S(2)}, u32[]{:S(2)}) collective-permute-start(bf16[576,6912]{1,0:T(8,128)(2,1)} %pad_maximum_fusion), channel_id=1, source_target_pairs={{0,4},{1,5},{2,6},{3,7},{4,0},{5,1},{6,2},{7,3},{8,12},{9,13},{10,... | collective-permute-start | bytes 23887880 | tf_op jit(solution)/shard_map/ppermute | solution.py:15
  811.6 222.9 %reduce-scatter.27.cloned.1.call-start = ((), (), s32[]{:S(2)}) async-start(), calls=%async_computation.18 | async-start | bytes 11943936 | tf_op jit(solution)/shard_map/reduce_scatter | solution.py:167
  827.1 368.9 %reduce-scatter.21.cloned.1.call-start = ((), (), s32[]{:S(2)}) async-start(), calls=%async_computation.15 | async-start | bytes 17915904 | tf_op jit(solution)/shard_map/reduce_scatter | solution.py:246
  866.9 368.3 %reduce-scatter.25.cloned.1.call-start = ((), (), s32[]{:S(2)}) async-start(), calls=%async_computation.17 | async-start | bytes 2985984 | tf_op jit(solution)/shard_map/reduce_scatter | solution.py:258
  870.2 452.3 %reduce-scatter.23.cloned.1.call-start = ((), (), s32[]{:S(2)}) async-start(), calls=%async_computation.16 | async-start | bytes 8957952 | tf_op jit(solution)/shard_map/reduce_scatter | solution.py:252
  877.2 476.8 %reduce-scatter.39.cloned.1.call-start = ((), (), s32[]{:S(2)}) async-start(), calls=%async_computation.27 | async-start | bytes 1843200
  925.8 469.6 %reduce-scatter.37.cloned.1.call-start = ((), (), s32[]{:S(2)}) async-start(), calls=%async_computation.26 | async-start | bytes 2949120
  1038.3 408.1 %reduce-scatter.31.cloned.1.call-start = ((), (), s32[]{:S(2)}) async-start(), calls=%async_computation.23 | async-start | bytes 4423680
  1200.6 300.3 %reduce-scatter.35.cloned.1.call-start = ((), (), s32[]{:S(2)}) async-start(), calls=%async_computation.25 | async-start | bytes 737280
  1237.2 383.7 %all-gather.20.cloned.1.call-start = ((), (), s32[]{:S(2)}) async-start(), calls=%async_computation.14 | async-start | bytes 17915904 | tf_op jit(solution)/shard_map/all_gather | solution.py:144
  1237.8 417.3 %reduce-scatter.33.cloned.1.call-start = ((), (), s32[]{:S(2)}) async-start(), calls=%async_computation.24 | async-start | bytes 2211840
  1325.1 364.3 %all-gather.24.cloned.1.call-start = ((), (), s32[]{:S(2)}) async-start(), calls=%async_computation.21 | async-start | bytes 1843200 | tf_op jit(solution)/shard_map/all_gather | solution.py:295
  1354.1 366.5 %all-gather.22.cloned.1.call-start = ((), (), s32[]{:S(2)}) async-start(), calls=%async_computation.19 | async-start | bytes 1658880 | tf_op jit(solution)/shard_map/all_gather | solution.py:292
  1397.4 360.5 %all-gather.26.cloned.1.call-start = ((), (), s32[]{:S(2)}) async-start(), calls=%async_computation.22 | async-start | bytes 2580480 | tf_op jit(solution)/shard_map/all_gather | solution.py:283
  1455.9 175.3 %copy-start.3 = (bf16[256,1152]{1,0:T(8,128)(2,1)}, bf16[256,1152]{1,0:T(8,128)(2,1)S(1)}, u32[]{:S(2)}) copy-start(bf16[256,1152]{1,0:T(8,128)(2,1)S(1)} %scatter_custom_fusion) | copy-start | bytes 1769476
  (42 other events, 1360.0 us)
Sparse Core Ops, SparseCore 0:
  9.7 111.6 all-gather.11
  123.0 54.4 all-gather.13
  179.2 341.6 all-gather.15
  522.3 141.4 all-gather.17
  811.8 111.3 reduce-scatter.28
  925.5 109.0 reduce-scatter.26
  1036.9 159.0 reduce-scatter.20
  1199.0 36.0 reduce-scatter.24
  1237.6 84.9 reduce-scatter.22
  1325.3 28.6 reduce-scatter.38
  1358.0 37.3 reduce-scatter.36
  1399.2 47.1 reduce-scatter.30
  1450.1 25.0 reduce-scatter.34
  1476.7 144.1 all-gather.19
  1624.3 30.6 reduce-scatter.32
  1656.8 32.5 all-gather.23
  1691.6 28.9 all-gather.21
  1722.9 35.0 all-gather.25
